TPU v7x, 128 devices: a whole 4x4x4 slice. The times are simulated.
128 devices in a mesh: outer: 16 (over z, x_lo, core), inner: 8 (over y, x_hi).
Axes of the slice: x: 4 (x_hi: 2, x_lo: 2; x = x_hi * 2 + x_lo), y: 4, z: 4, core: 2. Of those that a mesh axis runs over, the one named last changes fastest.
Arguments:
- queries: bfloat16 [8, 16384, 128], P(None, ('outer', 'inner')), may hold values from -6 to 6
- key_states: bfloat16 [16384, 128], P(('outer', 'inner')), may hold values from -6 to 6
- value_states: bfloat16 [16384, 128], P(('outer', 'inner')), may hold values from -6 to 6
- outputs: bfloat16 [8, 16384, 128], P(None, ('outer', 'inner')), may hold values from -6 to 6
- grad_outputs: bfloat16 [8, 16384, 128], P(None, ('outer', 'inner')), may hold values from -6 to 6
- log_sums: float32 [8, 16384], P(None, ('outer', 'inner')), may hold values from -1 to 20
- span_order: int32 [256], replicated, may hold values from 0 to 255, as said below
Outputs:
- query_grads: bfloat16 [8, 16384, 128], P(None, ('outer', 'inner'))
- key_grads: bfloat16 [16384, 128], P(('outer', 'inner'))
- value_grads: bfloat16 [16384, 128], P(('outer', 'inner'))
Inputs may be any that keep to these rules, and one draw needn't show every extreme that they name: span_order is a permutation of the 256 position blocks; entries 2 d and 2 d + 1 (the blocks stored on device d) add up to 255.
All inputs are finite; a program needn't handle non-finite values.
Results may differ from a plain program's by a relative error of at most 0.0052.
Values may be sent and summed in bfloat16 or wider, within the bound.
No kernel may reach another device: no remote copies, remote signals or barrier semaphores. Data moves between devices by JAX's collectives and lax.ppermute only.
A program may use at most 64 MiB of HBM per device.

v0:
```python
import math

import jax
import jax.numpy as jnp
from jax import lax
from jax.sharding import PartitionSpec as P


def sent_together(arrays, axis, dim, along):
    ends, at = ([], 0)
    for a in arrays[:-1]:
        at += a.shape[along]
        ends.append(at)
    both = jnp.concatenate(arrays, axis=along)
    return tuple(jnp.split(lax.all_gather(both, axis, axis=dim, tiled=True), ends, axis=along))


def split_up(shard, dim, peers):
    shape = shard.shape
    parts = shard.reshape(*shape[:dim], peers, shape[dim] // peers, *shape[dim + 1 :])
    return jnp.moveaxis(parts, dim, 0)


def summed_on_arrival(shard, axis, dim):
    peers = lax.axis_size(axis)
    parts = lax.all_to_all(split_up(shard, dim, peers), axis, 0, 0, tiled=True)
    return jnp.sum(parts, axis=0)


def table_lookup(table, indices):
    columns = jnp.arange(table.shape[0], dtype=jnp.int32)
    hits = indices[:, None] == columns[None, :]
    return jnp.sum(jnp.where(hits, table[None, :], 0), axis=1)


def row_positions(table, row_ids, span_rows):
    return table_lookup(table, row_ids // span_rows) * span_rows + row_ids % span_rows


def body(queries, key_states, value_states, outputs, grad_outputs, log_sums, span_order):
    head_count, row_count, head_width = queries.shape
    softmax_scale = 1.0 / math.sqrt(head_width)
    span_rows = row_count // 2
    query_rows = queries.reshape(head_count * row_count, head_width)
    grad_rows = grad_outputs.reshape(head_count * row_count, head_width)
    deltas = jnp.sum(
        grad_outputs.astype(jnp.float32) * outputs.astype(jnp.float32), axis=-1
    ).reshape(head_count * row_count, 1)
    log_norm = log_sums.reshape(head_count * row_count, 1)
    device_rank = lax.axis_index("outer") * lax.axis_size("inner") + lax.axis_index("inner")
    total_rows = row_count * lax.axis_size("outer") * lax.axis_size("inner")
    own_ids = device_rank * row_count + jnp.arange(row_count, dtype=jnp.int32)
    query_pos = row_positions(span_order, own_ids, span_rows)
    query_pos_rows = jnp.tile(query_pos, head_count)
    latest = jnp.max(query_pos)
    initial = (
        jnp.zeros((head_count * row_count, head_width), jnp.float32),
        jnp.zeros((total_rows, 2 * head_width), jnp.float32),
    )
    group_key, group_value = sent_together((key_states, value_states), "inner", 0, 1)
    key_piece, value_piece = sent_together((group_key, group_value), "outer", 0, 1)
    piece_rows = key_piece.shape[0]
    block_rows = 1024

    def one_block(step_index, state):
        local_start = step_index * block_rows
        key_block = lax.dynamic_slice_in_dim(key_piece, local_start, block_rows, 0)
        value_block = lax.dynamic_slice_in_dim(value_piece, local_start, block_rows, 0)
        key_ids = local_start + jnp.arange(block_rows, dtype=jnp.int32)
        key_pos = row_positions(span_order, key_ids, span_rows)

        def compute(inner_state):
            grad_query, grad_keys = inner_state
            scores = (
                jnp.dot(query_rows, key_block.T, preferred_element_type=jnp.float32) * softmax_scale
            )
            visible = query_pos_rows[:, None] >= key_pos[None, :]
            attend = jnp.where(visible, jnp.exp(scores - log_norm), 0.0)
            grad_prob = jnp.dot(grad_rows, value_block.T, preferred_element_type=jnp.float32)
            grad_score = attend * (grad_prob - deltas)
            attend_low = attend.astype(jnp.bfloat16)
            score_low = grad_score.astype(jnp.bfloat16)
            grad_query = (
                grad_query
                + jnp.dot(score_low, key_block, preferred_element_type=jnp.float32) * softmax_scale
            )
            key_part = (
                jnp.dot(score_low.T, query_rows, preferred_element_type=jnp.float32) * softmax_scale
            )
            value_part = jnp.dot(attend_low.T, grad_rows, preferred_element_type=jnp.float32)
            current = lax.dynamic_slice_in_dim(grad_keys, local_start, block_rows, 0)
            updated = current + jnp.concatenate([key_part, value_part], axis=1)
            grad_keys = lax.dynamic_update_slice_in_dim(grad_keys, updated, local_start, 0)
            return (grad_query, grad_keys)

        def unchanged(kept):
            return kept

        return lax.cond(latest >= jnp.min(key_pos), compute, unchanged, state)

    grad_query, grad_keys = lax.fori_loop(0, piece_rows // block_rows, one_block, initial)
    group_part = lax.psum_scatter(grad_keys, "outer", scatter_dimension=0, tiled=True)
    own_grads = summed_on_arrival(group_part, "inner", 0)
    query_grads = grad_query.reshape(head_count, row_count, head_width).astype(jnp.bfloat16)
    key_grads = own_grads[:, :head_width].astype(jnp.bfloat16)
    value_grads = own_grads[:, head_width:].astype(jnp.bfloat16)
    return (query_grads, key_grads, value_grads)


def solution(mesh):
    return jax.shard_map(
        body,
        mesh=mesh,
        in_specs=(
            P(None, ("outer", "inner"), None),
            P(("outer", "inner"), None),
            P(("outer", "inner"), None),
            P(None, ("outer", "inner"), None),
            P(None, ("outer", "inner"), None),
            P(None, ("outer", "inner")),
            P(),
        ),
        out_specs=(
            P(None, ("outer", "inner"), None),
            P(("outer", "inner"), None),
            P(("outer", "inner"), None),
        ),
        check_vma=False,
    )
```

profile of v0, /device:TPU:0, one launch (start us, length us, event | category | flops | bytes accessed | tf_op | source)
XLA Modules:
  0.0 518.8 jit_solution(2480716318308376656)
XLA Ops:
  8.0 37.8 %all_gather.6 = bf16[1024,256]{1,0:T(8,128)(2,1)} all-gather(bf16[128,256]{1,0:T(8,128)(2,1)S(1)} %pad_maximum_fusion), channel_id=1, replica_groups=mesh['outer'=16,'inner'=8] {'inner'}, dimensions={0}, use_global_device_ids=true | all-gather | bytes 589824 | tf_op jit(solution)/shard_map/all_gather | solution.py:15
  48.7 51.8 %all-gather.2.cloned.1.call-done = bf16[16384,256]{1,0:T(8,128)(2,1)} async-done(((bf16[1024,256]{1,0:T(8,128)(2,1)}), bf16[16384,256]{1,0:T(8,128)(2,1)}) %all-gather.2.cloned.1.call-update) | async-done | bytes 8388624 | tf_op jit(solution)/shard_map/all_gather | solution.py:15
  100.5 5.7 %fusion.29 = (bf16[16384,128]{1,0:T(8,128)(2,1)}, bf16[16384,128]{1,0:T(8,128)(2,1)}) fusion(bf16[16384,256]{1,0:T(8,128)(2,1)} %all-gather.2.cloned.1.call-done), kind=kLoop, calls=%fused_computation.50 | loop fusion | bytes 16777216 | tf_op jit(solution)/shard_map/split | solution.py:15
  106.3 6.0 %broadcast_in_dim.69 = f32[16384,256]{1,0:T(8,128)} broadcast(f32[]{:T(128)} %constant.171.clone.1), dimensions={} | broadcast | bytes 16777220 | tf_op jit(solution)/shard_map/broadcast_in_dim | solution.py:58
  112.3 193.5 %while.18 = (s32[]{:T(128)}, f32[1024,128]{1,0:T(8,128)S(1)}, f32[16384,256]{1,0:T(8,128)}, s32[256]{0:T(256)S(1)}, s32[]{:T(128)}, /*index=5*/bf16[16384,128]{1...) while((s32[]{:T(128)}, f32[1024,128]{1,0:T(8,128)S(1)}, ...), condition=%wide.region_8.9_spmd.clone, body=%wide.region_3.8_spmd.clone.sunk | while | flops 1356494848 | bytes 26007388 | solution.py:101
  114.7 9.8 %conditional.3 = ((f32[1024,128]{1,0:T(8,128)S(1)}, f32[16384,256]{1,0:T(8,128)})) conditional(s32[]{:T(128)} %convert_element_type.47, (f32[1024,128]{1,0:T(8,128)S(1)}, f32[16384,256]{1,0:T(8,128)}) %tuple.69, (s32[128]{0:T(128)S(1)}, s32[1024]{0:T(1024)S(1)}, s32[]{:T(128)}, bf16[16384,128]{1,0:T(8,128)(2,1)}, bf16[1024,128]{1,0:T(8,128)(2,1)S(1)}, ...), branch_computations={%region_6.6_spmd, %region_7.7_spmd} | conditional | flops 1355677696 | bytes 25985610 | solution.py:99
  126.7 9.8 %conditional.3 = ((f32[1024,128]{1,0:T(8,128)S(1)}, f32[16384,256]{1,0:T(8,128)})) conditional(s32[]{:T(128)} %convert_element_type.47, (f32[1024,128]{1,0:T(8,128)S(1)}, f32[16384,256]{1,0:T(8,128)}) %tuple.69, (s32[128]{0:T(128)S(1)}, s32[1024]{0:T(1024)S(1)}, s32[]{:T(128)}, bf16[16384,128]{1,0:T(8,128)(2,1)}, bf16[1024,128]{1,0:T(8,128)(2,1)S(1)}, ...), branch_computations={%region_6.6_spmd, %region_7.7_spmd} | conditional | flops 1355677696 | bytes 25985610 | solution.py:99
  138.9 9.8 %conditional.3 = ((f32[1024,128]{1,0:T(8,128)S(1)}, f32[16384,256]{1,0:T(8,128)})) conditional(s32[]{:T(128)} %convert_element_type.47, (f32[1024,128]{1,0:T(8,128)S(1)}, f32[16384,256]{1,0:T(8,128)}) %tuple.69, (s32[128]{0:T(128)S(1)}, s32[1024]{0:T(1024)S(1)}, s32[]{:T(128)}, bf16[16384,128]{1,0:T(8,128)(2,1)}, bf16[1024,128]{1,0:T(8,128)(2,1)S(1)}, ...), branch_computations={%region_6.6_spmd, %region_7.7_spmd} | conditional | flops 1355677696 | bytes 25985610 | solution.py:99
  150.9 9.8 %conditional.3 = ((f32[1024,128]{1,0:T(8,128)S(1)}, f32[16384,256]{1,0:T(8,128)})) conditional(s32[]{:T(128)} %convert_element_type.47, (f32[1024,128]{1,0:T(8,128)S(1)}, f32[16384,256]{1,0:T(8,128)}) %tuple.69, (s32[128]{0:T(128)S(1)}, s32[1024]{0:T(1024)S(1)}, s32[]{:T(128)}, bf16[16384,128]{1,0:T(8,128)(2,1)}, bf16[1024,128]{1,0:T(8,128)(2,1)S(1)}, ...), branch_computations={%region_6.6_spmd, %region_7.7_spmd} | conditional | flops 1355677696 | bytes 25985610 | solution.py:99
  163.0 9.8 %conditional.3 = ((f32[1024,128]{1,0:T(8,128)S(1)}, f32[16384,256]{1,0:T(8,128)})) conditional(s32[]{:T(128)} %convert_element_type.47, (f32[1024,128]{1,0:T(8,128)S(1)}, f32[16384,256]{1,0:T(8,128)}) %tuple.69, (s32[128]{0:T(128)S(1)}, s32[1024]{0:T(1024)S(1)}, s32[]{:T(128)}, bf16[16384,128]{1,0:T(8,128)(2,1)}, bf16[1024,128]{1,0:T(8,128)(2,1)S(1)}, ...), branch_computations={%region_6.6_spmd, %region_7.7_spmd} | conditional | flops 1355677696 | bytes 25985610 | solution.py:99
  175.1 9.8 %conditional.3 = ((f32[1024,128]{1,0:T(8,128)S(1)}, f32[16384,256]{1,0:T(8,128)})) conditional(s32[]{:T(128)} %convert_element_type.47, (f32[1024,128]{1,0:T(8,128)S(1)}, f32[16384,256]{1,0:T(8,128)}) %tuple.69, (s32[128]{0:T(128)S(1)}, s32[1024]{0:T(1024)S(1)}, s32[]{:T(128)}, bf16[16384,128]{1,0:T(8,128)(2,1)}, bf16[1024,128]{1,0:T(8,128)(2,1)S(1)}, ...), branch_computations={%region_6.6_spmd, %region_7.7_spmd} | conditional | flops 1355677696 | bytes 25985610 | solution.py:99
  187.2 9.8 %conditional.3 = ((f32[1024,128]{1,0:T(8,128)S(1)}, f32[16384,256]{1,0:T(8,128)})) conditional(s32[]{:T(128)} %convert_element_type.47, (f32[1024,128]{1,0:T(8,128)S(1)}, f32[16384,256]{1,0:T(8,128)}) %tuple.69, (s32[128]{0:T(128)S(1)}, s32[1024]{0:T(1024)S(1)}, s32[]{:T(128)}, bf16[16384,128]{1,0:T(8,128)(2,1)}, bf16[1024,128]{1,0:T(8,128)(2,1)S(1)}, ...), branch_computations={%region_6.6_spmd, %region_7.7_spmd} | conditional | flops 1355677696 | bytes 25985610 | solution.py:99
  199.3 9.8 %conditional.3 = ((f32[1024,128]{1,0:T(8,128)S(1)}, f32[16384,256]{1,0:T(8,128)})) conditional(s32[]{:T(128)} %convert_element_type.47, (f32[1024,128]{1,0:T(8,128)S(1)}, f32[16384,256]{1,0:T(8,128)}) %tuple.69, (s32[128]{0:T(128)S(1)}, s32[1024]{0:T(1024)S(1)}, s32[]{:T(128)}, bf16[16384,128]{1,0:T(8,128)(2,1)}, bf16[1024,128]{1,0:T(8,128)(2,1)S(1)}, ...), branch_computations={%region_6.6_spmd, %region_7.7_spmd} | conditional | flops 1355677696 | bytes 25985610 | solution.py:99
  211.4 9.9 %conditional.3 = ((f32[1024,128]{1,0:T(8,128)S(1)}, f32[16384,256]{1,0:T(8,128)})) conditional(s32[]{:T(128)} %convert_element_type.47, (f32[1024,128]{1,0:T(8,128)S(1)}, f32[16384,256]{1,0:T(8,128)}) %tuple.69, (s32[128]{0:T(128)S(1)}, s32[1024]{0:T(1024)S(1)}, s32[]{:T(128)}, bf16[16384,128]{1,0:T(8,128)(2,1)}, bf16[1024,128]{1,0:T(8,128)(2,1)S(1)}, ...), branch_computations={%region_6.6_spmd, %region_7.7_spmd} | conditional | flops 1355677696 | bytes 25985610 | solution.py:99
  223.6 9.8 %conditional.3 = ((f32[1024,128]{1,0:T(8,128)S(1)}, f32[16384,256]{1,0:T(8,128)})) conditional(s32[]{:T(128)} %convert_element_type.47, (f32[1024,128]{1,0:T(8,128)S(1)}, f32[16384,256]{1,0:T(8,128)}) %tuple.69, (s32[128]{0:T(128)S(1)}, s32[1024]{0:T(1024)S(1)}, s32[]{:T(128)}, bf16[16384,128]{1,0:T(8,128)(2,1)}, bf16[1024,128]{1,0:T(8,128)(2,1)S(1)}, ...), branch_computations={%region_6.6_spmd, %region_7.7_spmd} | conditional | flops 1355677696 | bytes 25985610 | solution.py:99
  235.6 9.8 %conditional.3 = ((f32[1024,128]{1,0:T(8,128)S(1)}, f32[16384,256]{1,0:T(8,128)})) conditional(s32[]{:T(128)} %convert_element_type.47, (f32[1024,128]{1,0:T(8,128)S(1)}, f32[16384,256]{1,0:T(8,128)}) %tuple.69, (s32[128]{0:T(128)S(1)}, s32[1024]{0:T(1024)S(1)}, s32[]{:T(128)}, bf16[16384,128]{1,0:T(8,128)(2,1)}, bf16[1024,128]{1,0:T(8,128)(2,1)S(1)}, ...), branch_computations={%region_6.6_spmd, %region_7.7_spmd} | conditional | flops 1355677696 | bytes 25985610 | solution.py:99
  247.7 9.8 %conditional.3 = ((f32[1024,128]{1,0:T(8,128)S(1)}, f32[16384,256]{1,0:T(8,128)})) conditional(s32[]{:T(128)} %convert_element_type.47, (f32[1024,128]{1,0:T(8,128)S(1)}, f32[16384,256]{1,0:T(8,128)}) %tuple.69, (s32[128]{0:T(128)S(1)}, s32[1024]{0:T(1024)S(1)}, s32[]{:T(128)}, bf16[16384,128]{1,0:T(8,128)(2,1)}, bf16[1024,128]{1,0:T(8,128)(2,1)S(1)}, ...), branch_computations={%region_6.6_spmd, %region_7.7_spmd} | conditional | flops 1355677696 | bytes 25985610 | solution.py:99
  259.8 9.8 %conditional.3 = ((f32[1024,128]{1,0:T(8,128)S(1)}, f32[16384,256]{1,0:T(8,128)})) conditional(s32[]{:T(128)} %convert_element_type.47, (f32[1024,128]{1,0:T(8,128)S(1)}, f32[16384,256]{1,0:T(8,128)}) %tuple.69, (s32[128]{0:T(128)S(1)}, s32[1024]{0:T(1024)S(1)}, s32[]{:T(128)}, bf16[16384,128]{1,0:T(8,128)(2,1)}, bf16[1024,128]{1,0:T(8,128)(2,1)S(1)}, ...), branch_computations={%region_6.6_spmd, %region_7.7_spmd} | conditional | flops 1355677696 | bytes 25985610 | solution.py:99
  271.9 9.8 %conditional.3 = ((f32[1024,128]{1,0:T(8,128)S(1)}, f32[16384,256]{1,0:T(8,128)})) conditional(s32[]{:T(128)} %convert_element_type.47, (f32[1024,128]{1,0:T(8,128)S(1)}, f32[16384,256]{1,0:T(8,128)}) %tuple.69, (s32[128]{0:T(128)S(1)}, s32[1024]{0:T(1024)S(1)}, s32[]{:T(128)}, bf16[16384,128]{1,0:T(8,128)(2,1)}, bf16[1024,128]{1,0:T(8,128)(2,1)S(1)}, ...), branch_computations={%region_6.6_spmd, %region_7.7_spmd} | conditional | flops 1355677696 | bytes 25985610 | solution.py:99
  284.0 9.8 %conditional.3 = ((f32[1024,128]{1,0:T(8,128)S(1)}, f32[16384,256]{1,0:T(8,128)})) conditional(s32[]{:T(128)} %convert_element_type.47, (f32[1024,128]{1,0:T(8,128)S(1)}, f32[16384,256]{1,0:T(8,128)}) %tuple.69, (s32[128]{0:T(128)S(1)}, s32[1024]{0:T(1024)S(1)}, s32[]{:T(128)}, bf16[16384,128]{1,0:T(8,128)(2,1)}, bf16[1024,128]{1,0:T(8,128)(2,1)S(1)}, ...), branch_computations={%region_6.6_spmd, %region_7.7_spmd} | conditional | flops 1355677696 | bytes 25985610 | solution.py:99
  296.1 9.8 %conditional.3 = ((f32[1024,128]{1,0:T(8,128)S(1)}, f32[16384,256]{1,0:T(8,128)})) conditional(s32[]{:T(128)} %convert_element_type.47, (f32[1024,128]{1,0:T(8,128)S(1)}, f32[16384,256]{1,0:T(8,128)}) %tuple.69, (s32[128]{0:T(128)S(1)}, s32[1024]{0:T(1024)S(1)}, s32[]{:T(128)}, bf16[16384,128]{1,0:T(8,128)(2,1)}, bf16[1024,128]{1,0:T(8,128)(2,1)S(1)}, ...), branch_computations={%region_6.6_spmd, %region_7.7_spmd} | conditional | flops 1355677696 | bytes 25985610 | solution.py:99
  305.9 183.6 %reduce-scatter.2.cloned.1.call-done = f32[1024,256]{1,0:T(8,128)} async-done(((f32[16384,256]{1,0:T(8,128)}), f32[1024,256]{1,0:T(8,128)}) %reduce-scatter.2.cloned.1.call-update) | async-done | bytes 1048592 | tf_op jit(solution)/shard_map/reduce_scatter | solution.py:102
  489.4 6.4 %all-to-all-start = ((f32[8,128,256]{2,1,0:T(8,128)}), f32[8,128,256]{2,1,0:T(8,128)S(1)}, u32[]{:S(2)}, u32[]{:S(2)}) async-start(f32[8,128,256]{2,1,0:T(8,128)} %bitcast.28), calls=%async_computation.1 | async-start | bytes 2097152 | tf_op jit(solution)/shard_map/all_to_all | solution.py:26
  496.6 14.7 %all-to-all-done = f32[8,128,256]{2,1,0:T(8,128)S(1)} async-done(((f32[8,128,256]{2,1,0:T(8,128)}), f32[8,128,256]{2,1,0:T(8,128)S(1)}, u32[]{:S(2)}, u32[]{:S(2)}) %all-to-all-start) | async-done | bytes 1048608 | tf_op jit(solution)/shard_map/all_to_all | solution.py:26
  (181 shorter events, 177.2 us)
Async XLA Ops:
  7.2 93.3 %all-gather.2.cloned.1.call-start = ((), (), s32[]{:S(2)}) async-start(), calls=%async_computation.2 | async-start | bytes 8912896 | tf_op jit(solution)/shard_map/all_gather | solution.py:15
  45.8 443.6 %reduce-scatter.2.cloned.1.call-start = ((), (), s32[]{:S(2)}) async-start(), calls=%async_computation.3 | async-start | bytes 17825792 | tf_op jit(solution)/shard_map/reduce_scatter | solution.py:102
  106.3 6.0 %copy-start = (bf16[8,128,128]{2,1,0:T(8,128)(2,1)S(1)}, bf16[8,128,128]{2,1,0:T(8,128)(2,1)}, u32[]{:S(2)}) copy-start(bf16[8,128,128]{2,1,0:T(8,128)(2,1)} %param.11) | copy-start | bytes 786436
  106.3 6.0 %copy-start.1 = (bf16[8,128,128]{2,1,0:T(8,128)(2,1)S(1)}, bf16[8,128,128]{2,1,0:T(8,128)(2,1)}, u32[]{:S(2)}) copy-start(bf16[8,128,128]{2,1,0:T(8,128)(2,1)} %param.15) | copy-start | bytes 786436
  106.3 6.0 %copy-start.2 = (s32[256]{0:T(256)S(1)}, s32[256]{0:T(256)}, u32[]{:S(2)}) copy-start(s32[256]{0:T(256)} %param.17) | copy-start | bytes 3076
  106.3 6.0 %copy-start.3 = (f32[8,128]{1,0:T(8,128)S(1)}, f32[8,128]{1,0:T(8,128)}, u32[]{:S(2)}) copy-start(f32[8,128]{1,0:T(8,128)} %param.16) | copy-start | bytes 12292
  489.4 21.9 %all-to-all-start = ((f32[8,128,256]{2,1,0:T(8,128)}), f32[8,128,256]{2,1,0:T(8,128)S(1)}, u32[]{:S(2)}, u32[]{:S(2)}) async-start(f32[8,128,256]{2,1,0:T(8,128)} %bitcast.28), calls=%async_computation.1 | async-start | bytes 2097152 | tf_op jit(solution)/shard_map/all_to_all | solution.py:26
Sparse Core Ops, SparseCore 0:
  46.0 54.5 all-gather.1
  306.0 183.3 reduce-scatter.1
where the time goes:
time: 522 us; the launch traced here: 519 us
  waiting for transfers between devices  250 us (48%)
  matrix products  118 us (23%)
  other arithmetic  58.5 us (11%)
  blocking collectives  37.8 us (7%)
  loops' own time  21.5 us (4%)
  between operations  14.1 us (3%)
  local copies, waits for them, and re-layouts  12.4 us (2%)
  starting transfers between devices  6.5 us (1%)
    reduce_scatter x1, waiting for transfers between devices, body(): lax.psum_scatter(grad_keys, 'outer', scatter_dimension=0, tiled=True)  184 us
    all_gather x1, waiting for transfers between devices, sent_together(): lax.all_gather(both, axis, axis=dim, tiled=True)  51.8 us
    all_gather x1, blocking collectives, sent_together(): lax.all_gather(both, axis, axis=dim, tiled=True)  37.8 us
    dynamic_update_slice x16, other arithmetic, compute(): lax.dynamic_update_slice_in_dim(grad_keys, updated, local_start, 0)  37.7 us
    dot_general x16, matrix products, compute(): jnp.dot(grad_rows, value_block.T, preferred_element_type=jnp.float32)  36.6 us
    dot_general x16, matrix products, compute(): jnp.dot(score_low, key_block, preferred_element_type=jnp.float32)  28.3 us
    dot_general x16, matrix products, compute(): jnp.dot(query_rows, key_block.T, preferred_element_type=jnp.float32)  26.6 us
    another operation x1, loops' own time, body(): lax.fori_loop(0, piece_rows // block_rows, one_block, initial)  20.5 us
  transfers between devices with their start and end apart: 3, of which 3 were waited for; matrix products, arithmetic and copies ran while one was open for 1% of the time, Pallas kernels for 0%

commit v1 on v0

v1 whole, which is shorter than its diff:
```python
import functools
import math

import jax
import jax.numpy as jnp
from jax import lax
from jax.experimental import pallas as pl
from jax.experimental.pallas import tpu as pltpu
from jax.sharding import Mesh
from jax.sharding import PartitionSpec as P

f32 = jnp.float32
bf16 = jnp.bfloat16
NT = (((1,), (1,)), ((), ()))
NN = (((1,), (0,)), ((), ()))
LOG2E = 1.0 / math.log(2.0)
AXES = ("z", "xl", "c", "y", "xh")
SIZES = (4, 2, 2, 4, 2)
WIDE = 4


def dot(a, b, dims):
    return lax.dot_general(a, b, dims, preferred_element_type=f32)


def kernel(
    first, scale, order, sorted_pos, query_block, below, own,
    qd_ref, st_ref, kv_ref, *rest,
):
    if first:
        dq_ref, dkv_ref, ks, vs, kt, dk, dv, dq = rest
    else:
        prev_ref, dq_ref, dkv_ref, ks, vs, kt, dk, dv, dq = rest
    groups, rows = qd_ref.shape[0], qd_ref.shape[2]
    blocks, span, _ = kv_ref.shape
    width = qd_ref.shape[3]
    chunk = WIDE * span
    for r in range(blocks):
        block = kv_ref[order[r]]
        ks[r * span : (r + 1) * span, :] = block[:, :width]
        vs[r * span : (r + 1) * span, :] = block[:, width:]
        if first:
            dk[r * span : (r + 1) * span, :] = jnp.zeros((span, width), f32)
            dv[r * span : (r + 1) * span, :] = jnp.zeros((span, width), f32)
        else:
            part = prev_ref[order[r]]
            dk[r * span : (r + 1) * span, :] = part[:, :width]
            dv[r * span : (r + 1) * span, :] = part[:, width:]
    for r in range(0, blocks * span, chunk):
        kt[:, r : r + chunk] = ks[r : r + chunk, :].T

    def unit(g, i, masked):
        at = pl.ds(pl.multiple_of(i * chunk, chunk), chunk)
        q, do = qd_ref[g, 0], qd_ref[g, 1]
        k, v = ks[at, :], vs[at, :]
        s = dot(k, q, NT)
        p = jnp.exp2(s * (scale * LOG2E) - st_ref[g, 0:1, :])
        if masked:
            lead = lax.rem(lax.broadcasted_iota(jnp.int32, (span, rows), 1), span)
            lead = lead - lax.broadcasted_iota(jnp.int32, (span, rows), 0)
            seen = [
                lead + (query_block[g] - sorted_pos[i * WIDE + j]) * span for j in range(WIDE)
            ]
            p = jnp.where(jnp.concatenate(seen, axis=0) >= 0, p, 0.0)
        dp = dot(v, do, NT)
        ds = (p * (dp - st_ref[g, 1:2, :])).astype(bf16)
        dv[at, :] += dot(p.astype(bf16), do, NN)
        dk[at, :] += dot(ds, q, NN)
        dq[...] += dot(kt[:, at], ds, NN)

    def group(g, carry):
        dq[...] = jnp.zeros_like(dq)
        whole = below[g] // WIDE

        def step(i, carry):
            unit(g, i, False)
            return carry

        lax.fori_loop(0, whole, step, 0)

        @pl.when(whole * WIDE < below[g] + own[g])
        def _():
            unit(g, whole, True)

        for j in range(0, rows, width):
            dq_ref[g, j : j + width, :] = dq[:, j : j + width].T.astype(dq_ref.dtype)
        return carry

    lax.fori_loop(0, groups, group, 0)
    for r in range(blocks):
        at = pl.ds(r * span, span)
        dkv_ref[order[r]] = jnp.concatenate([dk[at, :], dv[at, :]], axis=1).astype(dkv_ref.dtype)


def attend(tables, qd, st, kv, prev, dq_type, dkv_type, name):
    groups, _, rows, width = qd.shape
    blocks, span, _ = kv.shape
    vmem = pl.BlockSpec(memory_space=pltpu.VMEM)
    smem = pl.BlockSpec(memory_space=pltpu.SMEM)
    args = (qd, st, kv) + (() if prev is None else (prev,))
    scale = 1.0 / math.sqrt(width)
    pairs = groups * rows * blocks * span // 2
    return pl.pallas_call(
        functools.partial(kernel, prev is None, scale),
        out_shape=(
            jax.ShapeDtypeStruct((groups, rows, width), dq_type),
            jax.ShapeDtypeStruct(kv.shape, dkv_type),
        ),
        in_specs=[smem] * len(tables) + [vmem] * len(args),
        out_specs=(vmem, vmem),
        scratch_shapes=[
            pltpu.VMEM((blocks * span, width), bf16),
            pltpu.VMEM((blocks * span, width), bf16),
            pltpu.VMEM((width, blocks * span), bf16),
            pltpu.VMEM((blocks * span, width), f32),
            pltpu.VMEM((blocks * span, width), f32),
            pltpu.VMEM((width, rows), f32),
        ],
        cost_estimate=pl.CostEstimate(
            flops=pairs * width * 20, transcendentals=pairs, bytes_accessed=8 << 20
        ),
        compiler_params=pltpu.CompilerParams(vmem_limit_bytes=40 << 20),
        name=name,
    )(*tables, *args)


def lookup(table, ids):
    hits = ids[:, None] == jnp.arange(table.shape[0], dtype=jnp.int32)[None, :]
    return jnp.sum(jnp.where(hits, table[None, :], 0), axis=1)


def rank(z, xl, c, y, xh):
    return (((z * 2 + xl) * 2 + c) * 4 + y) * 2 + xh


def body(q, k, v, o, do, log_sums, span_order):
    heads, tokens, width = q.shape
    span = tokens // 2
    rows = heads * span
    scale = 1.0 / math.sqrt(width)
    z, xl, c, y, xh = [lax.axis_index(a) for a in AXES]

    kv = jnp.concatenate([k, v], axis=1)
    kv = lax.all_to_all(
        jnp.broadcast_to(kv[None], (16, tokens, 2 * width)), ("z", "y"), 0, 0, tiled=True
    ).reshape(32, span, 2 * width)

    def split(a):
        return a.reshape(heads, 2, span, width).transpose(1, 0, 2, 3).reshape(2, rows, width)

    qd = jnp.stack([split(q), split(do)], axis=1)
    delta = jnp.sum(do.astype(f32) * o.astype(f32), axis=-1)
    st = jnp.stack([log_sums * LOG2E, delta]).reshape(2, heads, 2, span)
    st = st.transpose(2, 0, 1, 3).reshape(2, 2, rows)
    qd = lax.all_to_all(
        jnp.broadcast_to(qd[None], (4, *qd.shape)), ("xl", "xh"), 0, 0, tiled=True
    ).reshape(8, 2, rows, width)
    st = lax.all_to_all(
        jnp.broadcast_to(st[None], (4, *st.shape)), ("xl", "xh"), 0, 0, tiled=True
    ).reshape(8, 2, rows)
    swap = [(0, 1), (1, 0)]
    qd_far = lax.ppermute(qd, "c", swap)
    st_far = lax.ppermute(st, "c", swap)

    i4 = jnp.arange(4, dtype=jnp.int32)
    i16 = jnp.arange(16, dtype=jnp.int32)
    kv_ids = rank(i16 // 4, xl, c, i16 % 4, xh)
    q_ids = jnp.concatenate([rank(z, i4 // 2, cc, y, i4 % 2) for cc in (c, 1 - c)])
    ids = jnp.concatenate([kv_ids, q_ids])
    ids = (ids[:, None] * 2 + jnp.arange(2, dtype=jnp.int32)[None, :]).reshape(48)
    pos = lookup(span_order, ids)
    kv_pos, q_pos = pos[:32], pos[32:]
    place = jnp.sum((kv_pos[None, :] < kv_pos[:, None]).astype(jnp.int32), axis=1)
    hit = place[:, None] == jnp.arange(32, dtype=jnp.int32)[None, :]
    order = jnp.sum(jnp.where(hit, jnp.arange(32, dtype=jnp.int32)[:, None], 0), axis=0)
    sorted_pos = jnp.sum(jnp.where(hit, kv_pos[:, None], 0), axis=0)
    below = jnp.sum((kv_pos[None, :] < q_pos[:, None]).astype(jnp.int32), axis=1)
    own = jnp.sum((kv_pos[None, :] == q_pos[:, None]).astype(jnp.int32), axis=1)

    near = (order, sorted_pos, q_pos[:8], below[:8], own[:8])
    far = (order, sorted_pos, q_pos[8:], below[8:], own[8:])
    dq_near, dkv = attend(near, qd, st, kv, None, f32, f32, "near")
    dq_far, dkv = attend(far, qd_far, st_far, kv, dkv, f32, bf16, "far")

    dkv = lax.all_to_all(dkv.reshape(16, tokens, 2 * width), ("z", "y"), 0, 0, tiled=True)
    dkv = jnp.sum(dkv.astype(f32), axis=0)
    dk = (dkv[:, :width] * scale).astype(bf16)
    dv = dkv[:, width:].astype(bf16)

    dq = (dq_near + lax.ppermute(dq_far, "c", swap)).astype(bf16)
    dq = lax.all_to_all(dq.reshape(4, 2, rows, width), ("xl", "xh"), 0, 0, tiled=True)
    dq = jnp.sum(dq.astype(f32), axis=0) * scale
    dq = dq.reshape(2, heads, span, width).transpose(1, 0, 2, 3).reshape(heads, tokens, width)
    return dq.astype(bf16), dk, dv


def solution(mesh):
    fine = Mesh(mesh.devices.reshape(SIZES), AXES)
    return jax.shard_map(
        body,
        mesh=fine,
        in_specs=(
            P(None, AXES, None),
            P(AXES, None),
            P(AXES, None),
            P(None, AXES, None),
            P(None, AXES, None),
            P(None, AXES),
            P(),
        ),
        out_specs=(P(None, AXES, None), P(AXES, None), P(AXES, None)),
        check_vma=False,
    )
```

time: 522 us -> 156 us (0.30)
  waiting for transfers between devices: 250 us -> 75.5 us
  matrix products: 118 us -> 0 us
  other arithmetic: 58.5 us -> 4.82 us
  Pallas kernels: 0 us -> 40.5 us
  blocking collectives: 37.8 us -> 0 us
  loops' own time: 21.5 us -> 0 us
  starting transfers between devices: 6.5 us -> 23.3 us
  between operations: 14.1 us -> 0.83 us
    reduce_scatter x1 -> x0, waiting for transfers between devices: 184 us -> none  [body(): lax.psum_scatter(grad_keys, 'outer', scatter_dimension=0, tiled=True)]
    dot_general x80 -> x0, matrix products: 118 us -> none  [the longest x16 36.6 us: compute(): jnp.dot(grad_rows, value_block.T, preferred_element_type=jnp.float32)]
    all_to_all x1 -> x5, waiting for transfers between devices: 14.7 us -> 74.7 us  [the longest x1 25.2 us: body(): lax.all_to_all(jnp.broadcast_to(qd[None], (4, *qd.shape)), ('xl', 'xh'),...]
    all_gather x1 -> x0, waiting for transfers between devices: 51.8 us -> none  [sent_together(): lax.all_gather(both, axis, axis=dim, tiled=True)]
    pallas_call x0 -> x2, Pallas kernels: none -> 40.5 us  [attend(): pl.pallas_call(functools.partial(kernel, prev is None, scale), out_shape=...]
    all_gather x1 -> x0, blocking collectives: 37.8 us -> none  [sent_together(): lax.all_gather(both, axis, axis=dim, tiled=True)]
    dynamic_update_slice x16 -> x0, other arithmetic: 37.7 us -> none  [compute(): lax.dynamic_update_slice_in_dim(grad_keys, updated, local_start, 0)]
    another operation x17 -> x0, loops' own time: 21.5 us -> none  [the longest x1 20.5 us: body(): lax.fori_loop(0, piece_rows // block_rows, one_block, initial)]
  transfers between devices with their start and end apart: 3 -> 8, of which waited for: 3 -> 6; matrix products, arithmetic and copies ran while one was open for 1% -> 4% of each run, Pallas kernels for 0% -> 12%
where the time goes in v1:
time: 156 us; the launch traced here: 155 us
  waiting for transfers between devices  75.5 us (48%)
  Pallas kernels  40.5 us (26%)
  starting transfers between devices  23.3 us (15%)
  local copies, waits for them, and re-layouts  9.75 us (6%)
  other arithmetic  4.82 us (3%)
    pallas_call x2, Pallas kernels, attend(): pl.pallas_call(functools.partial(kernel, prev is None, scale), out_shape=...  40.5 us
    all_to_all x1, waiting for transfers between devices, body(): lax.all_to_all(jnp.broadcast_to(qd[None], (4, *qd.shape)), ('xl', 'xh'),...  25.2 us
    all_to_all x1, waiting for transfers between devices, body(): lax.all_to_all(dkv.reshape(16, tokens, 2 * width), ('z', 'y'), 0, 0, tile...  15.7 us
    all_to_all x1, waiting for transfers between devices, body(): lax.all_to_all(jnp.broadcast_to(kv[None], (16, tokens, 2 * width)), ('z',...  15.6 us
    all_to_all x1, waiting for transfers between devices, body(): lax.all_to_all(dq.reshape(4, 2, rows, width), ('xl', 'xh'), 0, 0, tiled=T...  13.3 us
    all_to_all x1, starting transfers between devices, body(): lax.all_to_all(jnp.broadcast_to(kv[None], (16, tokens, 2 * width)), ('z',...  8.05 us
    all_to_all x1, waiting for transfers between devices, body(): lax.all_to_all(jnp.broadcast_to(st[None], (4, *st.shape)), ('xl', 'xh'),...  4.97 us
    all_to_all x1, starting transfers between devices, body(): lax.all_to_all(jnp.broadcast_to(qd[None], (4, *qd.shape)), ('xl', 'xh'),...  4.55 us
  transfers between devices with their start and end apart: 8, of which 6 were waited for; matrix products, arithmetic and copies ran while one was open for 4% of the time, Pallas kernels for 12%

profile of v1, /device:TPU:0, one launch (start us, length us, event | category | flops | bytes accessed | tf_op | source)
XLA Modules:
  0.0 154.6 jit_solution(2617654727068401169)
XLA Ops:
  0.6 1.0 copy.18
  1.6 1.0 copy.17
  2.7 1.8 %broadcast_in_dim.40 = bf16[4,2,2,512,128]{4,3,2,1,0:T(8,128)(2,1)} broadcast(bf16[2,2,512,128]{3,2,1,0:T(8,128)(2,1)S(1)} %copy.19), dimensions={1,2,3,4} | broadcast | bytes 2621440 | tf_op jit(solution)/shard_map/broadcast_in_dim | solution.py:156
  4.5 4.5 %all-to-all-start = ((bf16[4,2,2,512,128]{4,3,2,1,0:T(8,128)(2,1)}), bf16[4,2,2,512,128]{4,3,2,1,0:T(8,128)(2,1)S(1)}, u32[]{:S(2)}, u32[]{:S(2)}) async-start(bf16[4,2,2,512,128]{4,3,2,1,0:T(8,128)(2,1)} %broadcast_in_dim.40), calls=%async_computation | async-start | bytes 4194304 | tf_op jit(solution)/shard_map/all_to_all | solution.py:155
  9.8 25.2 %all-to-all-done = bf16[4,2,2,512,128]{4,3,2,1,0:T(8,128)(2,1)S(1)} async-done(((bf16[4,2,2,512,128]{4,3,2,1,0:T(8,128)(2,1)}), bf16[4,2,2,512,128]{4,3,2,1,0:T(8,128)(2,1)S(1)}, u32[]{:S(2)}, u32[]{:S(2)}) %all-to-all-start) | async-done | bytes 2097184 | tf_op jit(solution)/shard_map/all_to_all | solution.py:155
  35.1 0.6 broadcast_in_dim.67
  35.7 3.3 %all-to-all-start.1 = ((f32[4,2,2,512]{3,2,1,0:T(2,128)}), f32[4,2,2,512]{3,2,1,0:T(2,128)S(1)}, u32[]{:S(2)}, u32[]{:S(2)}) async-start(f32[4,2,2,512]{3,2,1,0:T(2,128)} %broadcast_in_dim.67), calls=%async_computation.1 | async-start | bytes 65536 | tf_op jit(solution)/shard_map/all_to_all | solution.py:158
  39.3 5.0 %all-to-all-done.1 = f32[4,2,2,512]{3,2,1,0:T(2,128)S(1)} async-done(((f32[4,2,2,512]{3,2,1,0:T(2,128)}), f32[4,2,2,512]{3,2,1,0:T(2,128)S(1)}, u32[]{:S(2)}, u32[]{:S(2)}) %all-to-all-start.1) | async-done | bytes 32800 | tf_op jit(solution)/shard_map/all_to_all | solution.py:158
  44.3 1.1 broadcast_in_dim.68
  45.3 8.0 %all-to-all-start.2 = ((bf16[16,128,256]{2,1,0:T(8,128)(2,1)}), bf16[16,128,256]{2,1,0:T(8,128)(2,1)S(1)}, u32[]{:S(2)}, u32[]{:S(2)}) async-start(bf16[16,128,256]{2,1,0:T(8,128)(2,1)} %broadcast_in_dim.68), calls=%async_computation.2 | async-start | bytes 2097152 | tf_op jit(solution)/shard_map/all_to_all | solution.py:144
  54.1 15.6 %all-to-all-done.2 = bf16[16,128,256]{2,1,0:T(8,128)(2,1)S(1)} async-done(((bf16[16,128,256]{2,1,0:T(8,128)(2,1)}), bf16[16,128,256]{2,1,0:T(8,128)(2,1)S(1)}, u32[]{:S(2)}, u32[]{:S(2)}) %all-to-all-start.2) | async-done | bytes 1048608 | tf_op jit(solution)/shard_map/all_to_all | solution.py:144
  69.6 18.9 %near.1 = (f32[8,512,128]{2,1,0:T(8,128)S(1)}, f32[32,64,256]{2,1,0:T(8,128)S(1)}) custom-call(s32[32]{0:T(128)S(1)} %get-tuple-element.14.order, s32[32]{0:T(128)S(1)} %get-tuple-element.13.sorted_pos, s32[8]{0:T(128)S(1)} %get-tuple-element.20.query_block, s32[8]{0:T(128)S(1)} %get-tuple-element.18.below, s32[8]{0:T(128)S(1)} %get-tuple-element.16.own, ...), custom_call_target="tpu_custom_call" | custom-call | flops 10737418240 | bytes 8388608 | tf_op jit(solution)/shard_map/near/pallas_call | solution.py:103
  88.5 1.3 copy-done
  89.9 21.6 %far.1 = (f32[8,512,128]{2,1,0:T(8,128)}, bf16[32,64,256]{2,1,0:T(8,128)(2,1)S(1)}) custom-call(s32[32]{0:T(128)S(1)} %get-tuple-element.14.order, s32[32]{0:T(128)S(1)} %get-tuple-element.13.sorted_pos, s32[8]{0:T(128)S(1)} %get-tuple-element.19.query_block, s32[8]{0:T(128)S(1)} %get-tuple-element.17.below, s32[8]{0:T(128)S(1)} %get-tuple-element.15.own, ...), custom_call_target="tpu_custom_call" | custom-call | flops 10737418240 | bytes 8388608 | tf_op jit(solution)/shard_map/far/pallas_call | solution.py:103
  111.5 1.0 copy-done.2
  112.5 3.8 %all-to-all-start.4 = ((bf16[16,128,256]{2,1,0:T(8,128)(2,1)}), bf16[16,128,256]{2,1,0:T(8,128)(2,1)S(1)}, u32[]{:S(2)}, u32[]{:S(2)}) async-start(bf16[16,128,256]{2,1,0:T(8,128)(2,1)} %bitcast.26), calls=%async_computation.4 | async-start | bytes 2097152 | tf_op jit(solution)/shard_map/all_to_all | solution.py:185
  116.3 0.7 collective-permute-done.2
  117.0 2.8 %add_convert_fusion = bf16[8,512,128]{2,1,0:T(8,128)(2,1)} fusion(f32[8,512,128]{2,1,0:T(8,128)S(1)} %copy-done.1, f32[8,512,128]{2,1,0:T(8,128)} %collective-permute-done.2), kind=kLoop, calls=%fused_computation.2 | loop fusion | flops 1048576 | bytes 5242880 | tf_op jit(solution)/shard_map/convert_element_type | solution.py:190
  119.7 15.7 %all-to-all-done.4 = bf16[16,128,256]{2,1,0:T(8,128)(2,1)S(1)} async-done(((bf16[16,128,256]{2,1,0:T(8,128)(2,1)}), bf16[16,128,256]{2,1,0:T(8,128)(2,1)S(1)}, u32[]{:S(2)}, u32[]{:S(2)}) %all-to-all-start.4) | async-done | bytes 1048608 | tf_op jit(solution)/shard_map/all_to_all | solution.py:185
  135.4 3.5 %all-to-all-start.3 = ((bf16[4,2,512,128]{3,2,1,0:T(8,128)(2,1)}), bf16[4,2,512,128]{3,2,1,0:T(8,128)(2,1)S(1)}, u32[]{:S(2)}, u32[]{:S(2)}) async-start(bf16[4,2,512,128]{3,2,1,0:T(8,128)(2,1)} %bitcast.10), calls=%async_computation.3 | async-start | bytes 2097152 | tf_op jit(solution)/shard_map/all_to_all | solution.py:191
  139.1 0.6 slice.49
  139.7 0.6 fusion
  140.3 13.3 %all-to-all-done.3 = bf16[4,2,512,128]{3,2,1,0:T(8,128)(2,1)S(1)} async-done(((bf16[4,2,512,128]{3,2,1,0:T(8,128)(2,1)}), bf16[4,2,512,128]{3,2,1,0:T(8,128)(2,1)S(1)}, u32[]{:S(2)}, u32[]{:S(2)}) %all-to-all-start.3) | async-done | bytes 1048608 | tf_op jit(solution)/shard_map/all_to_all | solution.py:191
  153.9 0.7 copy.21
  (47 shorter events, 2.2 us)
Async XLA Ops:
  4.4 4.9 %copy-start.3 = (bf16[8,128,128]{2,1,0:T(8,128)(2,1)S(1)}, bf16[8,128,128]{2,1,0:T(8,128)(2,1)}, u32[]{:S(2)}) copy-start(bf16[8,128,128]{2,1,0:T(8,128)(2,1)} %param.11) | copy-start | bytes 786436
  4.4 4.9 %copy-start.4 = (bf16[8,128,128]{2,1,0:T(8,128)(2,1)S(1)}, bf16[8,128,128]{2,1,0:T(8,128)(2,1)}, u32[]{:S(2)}) copy-start(bf16[8,128,128]{2,1,0:T(8,128)(2,1)} %param.10) | copy-start | bytes 786436
  4.4 5.2 %copy-start.7 = (f32[8,128]{1,0:T(8,128)S(1)}, f32[8,128]{1,0:T(8,128)}, u32[]{:S(2)}) copy-start(f32[8,128]{1,0:T(8,128)} %param.12) | copy-start | bytes 12292
  4.4 5.4 %copy-start.5 = (bf16[128,128]{1,0:T(8,128)(2,1)S(1)}, bf16[128,128]{1,0:T(8,128)(2,1)}, u32[]{:S(2)}) copy-start(bf16[128,128]{1,0:T(8,128)(2,1)} %param.9) | copy-start | bytes 98308
  4.4 5.4 %copy-start.6 = (bf16[128,128]{1,0:T(8,128)(2,1)S(1)}, bf16[128,128]{1,0:T(8,128)(2,1)}, u32[]{:S(2)}) copy-start(bf16[128,128]{1,0:T(8,128)(2,1)} %param.8) | copy-start | bytes 98308
  4.5 34.6 %copy-start.8 = (s32[256]{0:T(256)S(1)}, s32[256]{0:T(256)}, u32[]{:S(2)}) copy-start(s32[256]{0:T(256)} %param.13) | copy-start | bytes 3076
  4.5 30.6 %all-to-all-start = ((bf16[4,2,2,512,128]{4,3,2,1,0:T(8,128)(2,1)}), bf16[4,2,2,512,128]{4,3,2,1,0:T(8,128)(2,1)S(1)}, u32[]{:S(2)}, u32[]{:S(2)}) async-start(bf16[4,2,2,512,128]{4,3,2,1,0:T(8,128)(2,1)} %broadcast_in_dim.40), calls=%async_computation | async-start | bytes 4194304 | tf_op jit(solution)/shard_map/all_to_all | solution.py:155
  35.7 8.6 %all-to-all-start.1 = ((f32[4,2,2,512]{3,2,1,0:T(2,128)}), f32[4,2,2,512]{3,2,1,0:T(2,128)S(1)}, u32[]{:S(2)}, u32[]{:S(2)}) async-start(f32[4,2,2,512]{3,2,1,0:T(2,128)} %broadcast_in_dim.67), calls=%async_computation.1 | async-start | bytes 65536 | tf_op jit(solution)/shard_map/all_to_all | solution.py:158
  39.0 50.9 %collective-permute-start = (bf16[8,2,512,128]{3,2,1,0:T(8,128)(2,1)S(1)}, bf16[8,2,512,128]{3,2,1,0:T(8,128)(2,1)}, u32[]{:S(2)}, u32[]{:S(2)}) collective-permute-start(bf16[8,2,512,128]{3,2,1,0:T(8,128)(2,1)S(1)} %bitcast.22), channel_id=1, source_target_pairs={{0,8},{8,0},{1,9},{9,1},{2,10},{10,2},{3,11},{11,3},{4,12},{12,4},... | collective-permute-start | bytes 6291464 | tf_op jit(solution)/shard_map/ppermute | solution.py:162
  45.3 24.3 %all-to-all-start.2 = ((bf16[16,128,256]{2,1,0:T(8,128)(2,1)}), bf16[16,128,256]{2,1,0:T(8,128)(2,1)S(1)}, u32[]{:S(2)}, u32[]{:S(2)}) async-start(bf16[16,128,256]{2,1,0:T(8,128)(2,1)} %broadcast_in_dim.68), calls=%async_computation.2 | async-start | bytes 2097152 | tf_op jit(solution)/shard_map/all_to_all | solution.py:144
  54.1 35.8 %collective-permute-start.1 = (f32[8,2,512]{2,1,0:T(2,128)S(1)}, f32[8,2,512]{2,1,0:T(2,128)S(1)}, u32[]{:S(2)}, u32[]{:S(2)}) collective-permute-start(f32[8,2,512]{2,1,0:T(2,128)S(1)} %bitcast.27), channel_id=1, source_target_pairs={{0,8},{8,0},{1,9},{9,1},{2,10},{10,2},{3,11},{11,3},{4,12},{12,4},... | collective-permute-start | bytes 98312 | tf_op jit(solution)/shard_map/ppermute | solution.py:163
  88.5 1.3 copy-start
  111.5 1.0 copy-start.2
  112.5 4.5 %copy-start.1 = (f32[8,512,128]{2,1,0:T(8,128)S(1)}, f32[8,512,128]{2,1,0:T(8,128)}, u32[]{:S(2)}) copy-start(f32[8,512,128]{2,1,0:T(8,128)} %copy-done) | copy-start | bytes 6291460
  112.5 4.5 %collective-permute-start.2 = (f32[8,512,128]{2,1,0:T(8,128)}, f32[8,512,128]{2,1,0:T(8,128)}, u32[]{:S(2)}, u32[]{:S(2)}) collective-permute-start(f32[8,512,128]{2,1,0:T(8,128)} %get-tuple-element.9), channel_id=1, source_target_pairs={{0,8},{8,0},{1,9},{9,1},{2,10},{10,2},{3,11},{11,3},{4,12},{12,4},... | collective-permute-start | bytes 6291464 | tf_op jit(solution)/shard_map/ppermute | solution.py:190
  112.5 22.9 %all-to-all-start.4 = ((bf16[16,128,256]{2,1,0:T(8,128)(2,1)}), bf16[16,128,256]{2,1,0:T(8,128)(2,1)S(1)}, u32[]{:S(2)}, u32[]{:S(2)}) async-start(bf16[16,128,256]{2,1,0:T(8,128)(2,1)} %bitcast.26), calls=%async_computation.4 | async-start | bytes 2097152 | tf_op jit(solution)/shard_map/all_to_all | solution.py:185
  135.4 18.3 %all-to-all-start.3 = ((bf16[4,2,512,128]{3,2,1,0:T(8,128)(2,1)}), bf16[4,2,512,128]{3,2,1,0:T(8,128)(2,1)S(1)}, u32[]{:S(2)}, u32[]{:S(2)}) async-start(bf16[4,2,512,128]{3,2,1,0:T(8,128)(2,1)} %bitcast.10), calls=%async_computation.3 | async-start | bytes 2097152 | tf_op jit(solution)/shard_map/all_to_all | solution.py:191
